TPU v7x, 256 devices: a whole 4x4x8 slice. The times are simulated.
256 devices in a mesh: cols: 64 (over z, y_lo, x), par: 4 (over y_hi, core).
Axes of the slice: x: 4, y: 4 (y_hi: 2, y_lo: 2; y = y_hi * 2 + y_lo), z: 8, core: 2. Of those that a mesh axis runs over, the one named last changes fastest.
Arguments:
- tile_bounds: int32 [65], replicated, may hold values from 0 to 16384, as said below
- tile_anchor: int32 [512, 2], P(('cols', 'par')), may hold values from 0 to 256, as said below
- tile_picks: int32 [512], P(('cols', 'par')), may hold values from 16 to 64, as said below
- rmo_picks: bfloat16 [512, 64], P(('cols', 'par')), may hold values from -6 to 6
- sensitivity: bfloat16 [512, 64, 3, 16, 128], P(('cols', 'par')), may hold values from -0.75 to 0.75
- dip_class: int32 [256, 64, 256], P(('cols', 'par')), may hold values from 0 to 8
- strength: float32 [3], replicated, may hold values from 0.05 to 0.2
- couple: float32 [3, 3], replicated, may hold values from 0.1 to 1
Outputs:
- model_update: float32 [3, 256, 64, 256], P(None, ('cols', 'par'))
Inputs may be any that keep to these rules, and one draw needn't show every extreme that they name: tile_bounds[0] = 0 and tile_bounds[64] = 16384; column tile c holds grid columns tile_bounds[c] to tile_bounds[c + 1] - 1, between 128 and 384 of them, and some column tile holds exactly 384. Fat-ray tile t belongs to column tile t // (2 * 4); it covers depth cells tile_anchor[t, 0] to tile_anchor[t, 0] + 15 and column slots tile_anchor[t, 1] to tile_anchor[t, 1] + 127 of that column tile, all of them among its columns and within the grid. Rays 0 to tile_picks[t] - 1 of tile t are live; some tile has 64 live rays.
All inputs are finite; a program needn't handle non-finite values.
Results may differ from a plain program's by a relative error of at most 0.0003.
Values sent between devices are 32-bit elements; how exact they have to be, the bound alone decides.
A program may use at most 192 MiB of HBM per device.

v0:
```python
import jax
import jax.numpy as jnp
from jax import lax
from jax.sharding import PartitionSpec as P

CAP = 384
PASSES = 6


def extended(block, sides, width):
    for axis, dim in sides:
        count = lax.axis_size(axis)
        forward = [(i, i + 1) for i in range(count - 1)]
        backward = [(target, source) for source, target in forward]
        low = lax.ppermute(
            lax.slice_in_dim(block, block.shape[dim] - width, None, axis=dim), axis, forward
        )
        high = lax.ppermute(lax.slice_in_dim(block, 0, width, axis=dim), axis, backward)
        block = jnp.concatenate([low, block, high], axis=dim)
    return block


def next_cells(values, along_dim):
    count = values.shape[along_dim]
    kept = lax.slice_in_dim(values, 1, count, axis=along_dim)
    zeros = jnp.zeros_like(lax.slice_in_dim(values, 0, 1, axis=along_dim))
    return jnp.concatenate([kept, zeros], axis=along_dim)


def prev_cells(values, along_dim):
    count = values.shape[along_dim]
    kept = lax.slice_in_dim(values, 0, count - 1, axis=along_dim)
    zeros = jnp.zeros_like(lax.slice_in_dim(values, 0, 1, axis=along_dim))
    return jnp.concatenate([zeros, kept], axis=along_dim)


def at_depth(padded, tilt):
    return jnp.where(tilt < 0, padded[:, :-2], jnp.where(tilt > 0, padded[:, 2:], padded[:, 1:-1]))


def smooth_pass(padded, dip_class, strength, mixing):
    centre = padded[:, 1:-1]
    tilt_across = (dip_class // 3 - 1)[None]
    tilt_along = (dip_class % 3 - 1)[None]
    east_side = at_depth(next_cells(padded, 2), tilt_across)
    west_side = at_depth(prev_cells(padded, 2), -tilt_across)
    north_side = at_depth(next_cells(padded, 3), tilt_along)
    south_side = at_depth(prev_cells(padded, 3), -tilt_along)
    laplace = east_side + west_side + north_side + south_side - 4.0 * centre
    smooth = centre + strength[:, None, None, None] * laplace
    return jnp.tensordot(mixing, smooth, axes=1, precision=lax.Precision.HIGHEST)


def shards(
    tile_bounds, tile_anchor, tile_picks, rmo_picks, sensitivity, dip_class, strength, couple
):
    tile_count, ray_count, param_count, depth_cells, tile_columns = sensitivity.shape
    col_devices = lax.axis_size("cols")
    par_devices = lax.axis_size("par")
    slab_depth, rows_x, rows_y = dip_class.shape
    total_depth = slab_depth * col_devices * par_devices
    live = jnp.arange(ray_count, dtype=jnp.int32)[None, :] < tile_picks[:, None]
    ray_weight = jnp.where(live, rmo_picks, jnp.zeros_like(rmo_picks))
    contribution = jnp.einsum(
        "tr,trk->tk",
        ray_weight,
        sensitivity.reshape(tile_count, ray_count, -1),
        preferred_element_type=jnp.float32,
    )
    contribution = contribution.reshape(tile_count, param_count, depth_cells, tile_columns)

    def add_tile(tile_number, gradient):
        anchor = (jnp.int32(0), tile_anchor[tile_number, 0], tile_anchor[tile_number, 1])
        current = lax.dynamic_slice(gradient, anchor, (param_count, depth_cells, tile_columns))
        return lax.dynamic_update_slice(gradient, current + contribution[tile_number], anchor)

    gradient = jnp.zeros((param_count, total_depth, CAP), jnp.float32)
    gradient = lax.fori_loop(0, tile_count, add_tile, gradient)
    blocks = gradient.reshape(param_count, col_devices, par_devices, slab_depth, CAP)
    moved = lax.all_to_all(blocks, "cols", split_axis=1, concat_axis=4, tiled=True)
    summed = lax.psum_scatter(moved, "par", scatter_dimension=2, tiled=True)
    padded_slots = summed.reshape(param_count, slab_depth, col_devices * CAP)
    columns = rows_x * rows_y
    column_ids = jnp.arange(columns, dtype=jnp.int32)
    starts = tile_bounds[:-1]
    below = starts[None, :] <= column_ids[:, None]
    owner_tile = jnp.sum(below.astype(jnp.int32), axis=1) - 1
    tile_start = jnp.max(jnp.where(below, starts[None, :], jnp.zeros_like(starts)[None, :]), axis=1)
    slot_index = owner_tile * CAP + column_ids - tile_start
    field = jnp.take(padded_slots, slot_index, axis=2).reshape(
        param_count, slab_depth, rows_x, rows_y
    )
    mixing = couple / jnp.sum(couple, axis=1, keepdims=True)
    for _ in range(PASSES):
        padded = extended(field, ((("cols", "par"), 1),), 1)
        field = smooth_pass(padded, dip_class, strength, mixing)
    return field


def solution(mesh):
    return jax.shard_map(
        shards,
        mesh=mesh,
        in_specs=(
            P(),
            P(("cols", "par"), None),
            P(("cols", "par")),
            P(("cols", "par"), None),
            P(("cols", "par"), None, None, None, None),
            P(("cols", "par"), None, None),
            P(),
            P(),
        ),
        out_specs=P(None, ("cols", "par"), None, None),
        check_vma=False,
    )
```

profile of v0, /device:TPU:32, one launch (start us, length us, event | category | flops | bytes accessed | tf_op | source)
XLA Modules:
  0.0 618.3 jit_solution(5510151332754518831)
XLA Ops:
  6.5 2.5 reshape.224
  9.8 12.1 %while.13 = (s32[]{:T(128)}, f32[3,256,384]{2,1,0:T(8,128)S(1)}, s32[2,2]{1,0:T(2,128)S(1)}, f32[2,3,16,128]{3,2,1,0:T(8,128)S(1)}, s32[]{:T(128)}, /*index=5*/s32[]{:T(128)}, s32[]{:T(128)}, s32[]{:T(128)}) while((s32[]{:T(128)}, f32[3,256,384]{2,1,0:T(8,128)S(1)}, s32[2,2]{1,0:T(2,128)S(1)}, f32[2,3,16,128]{3,2,1,0:T(8,128)S(1)}, s32[]{:T(128)}, ...), condition=%wide.region_4.5_spmd, body=%wide.region_3.4_spmd.sunk | while | flops 6152 | bytes 123077 | solution.py:78
  9.8 0.6 constant_dynamic-slice_fusion.3
  14.2 1.6 dynamic_update_slice.8
  15.8 0.6 constant_dynamic-slice_fusion.3
  20.3 1.6 dynamic_update_slice.8
  22.2 1.2 copy.24
  23.5 12.7 %all-to-all-start = ((f32[3,64,4,1,384]{4,2,3,0,1:T(4,128)}), f32[3,64,4,1,384]{4,2,3,0,1:T(4,128)S(1)}, u32[]{:S(2)}, u32[]{:S(2)}) async-start(f32[3,64,4,1,384]{4,2,3,0,1:T(4,128)} %copy.24), calls=%async_computation | async-start | bytes 2359296 | tf_op jit(solution)/shard_map/all_to_all | solution.py:80
  36.3 1.3 convert_reduce_fusion
  37.6 29.0 %all-to-all-done = f32[3,64,4,1,384]{4,2,3,0,1:T(4,128)S(1)} async-done(((f32[3,64,4,1,384]{4,2,3,0,1:T(4,128)}), f32[3,64,4,1,384]{4,2,3,0,1:T(4,128)S(1)}, u32[]{:S(2)}, u32[]{:S(2)}) %all-to-all-start) | async-done | bytes 1179680 | tf_op jit(solution)/shard_map/all_to_all | solution.py:80
  66.5 23.2 %copy.25 = f32[3,1,4,1,64,384]{0,5,4,2,3,1:T(8,128)} copy(f32[3,1,4,1,64,384]{5,2,0,4,3,1:T(4,128)S(1)} %bitcast.134) | data formatting | bytes 2359296 | tf_op jit(solution)/shard_map/all_to_all | solution.py:80
  90.8 355.7 %reduce-scatter.2.cloned.1.call-done = f32[3,1,1,1,24576]{0,4,3,2,1:T(8,128)} async-done(((f32[3,1,4,1,24576]{0,4,3,2,1:T(8,128)}), f32[3,1,1,1,24576]{0,4,3,2,1:T(8,128)}) %reduce-scatter.2.cloned.1.call-update) | async-done | bytes 294928 | tf_op jit(solution)/shard_map/reduce_scatter | solution.py:81
  446.5 59.1 %gather_fusion = f32[16384,3]{1,0:T(8,128)} fusion(f32[3,24576]{0,1:T(8,128)} %bitcast.138, s32[16384]{0:T(1024)S(1)} %broadcast_clamp_fusion), kind=kCustom, calls=%fused_computation | custom fusion | bytes 458752 | tf_op jit(solution)/shard_map/jit(_take)/gather | solution.py:90
  505.5 5.3 copy.27
  511.0 4.4 collective-permute-start.1
  515.4 1.9 collective-permute-start
  517.4 1.9 collective-permute-done.1
  519.3 8.0 %collective-permute-done = f32[3,1,64,256]{3,0,2,1:T(4,128)S(1)} collective-permute-done((f32[3,1,64,256]{3,0,2,1:T(4,128)S(1)}, f32[3,1,64,256]{3,0,2,1:T(4,128)S(1)}, u32[]{:S(2)}, u32[]{:S(2)}) %collective-permute-start) | collective-permute-done | bytes 196640 | tf_op jit(solution)/shard_map/ppermute | solution.py:15
  527.5 0.5 fusion.202
  528.7 1.3 fusion.93
  530.0 1.9 collective-permute-start.3
  531.9 2.4 collective-permute-start.2
  534.3 1.5 collective-permute-done.3
  535.8 8.0 %collective-permute-done.2 = f32[3,1,64,256]{3,0,2,1:T(4,128)S(1)} collective-permute-done((f32[3,1,64,256]{3,0,2,1:T(4,128)S(1)}, f32[3,1,64,256]{3,0,2,1:T(4,128)S(1)}, u32[]{:S(2)}, u32[]{:S(2)}) %collective-permute-start.2) | collective-permute-done | bytes 196640 | tf_op jit(solution)/shard_map/ppermute | solution.py:15
  544.0 0.5 fusion.200
  544.7 1.3 fusion.91
  546.0 2.0 collective-permute-start.5
  548.0 2.5 collective-permute-start.4
  550.6 1.3 collective-permute-done.5
  551.9 8.0 %collective-permute-done.4 = f32[3,1,64,256]{3,0,2,1:T(4,128)S(1)} collective-permute-done((f32[3,1,64,256]{3,0,2,1:T(4,128)S(1)}, f32[3,1,64,256]{3,0,2,1:T(4,128)S(1)}, u32[]{:S(2)}, u32[]{:S(2)}) %collective-permute-start.4) | collective-permute-done | bytes 196640 | tf_op jit(solution)/shard_map/ppermute | solution.py:15
  560.9 1.3 fusion.89
  562.2 2.0 collective-permute-start.7
  564.2 2.3 collective-permute-start.6
  566.5 1.5 collective-permute-done.7
  568.1 8.0 %collective-permute-done.6 = f32[3,1,64,256]{3,0,2,1:T(4,128)S(1)} collective-permute-done((f32[3,1,64,256]{3,0,2,1:T(4,128)S(1)}, f32[3,1,64,256]{3,0,2,1:T(4,128)S(1)}, u32[]{:S(2)}, u32[]{:S(2)}) %collective-permute-start.6) | collective-permute-done | bytes 196640 | tf_op jit(solution)/shard_map/ppermute | solution.py:15
  577.0 1.3 fusion.87
  578.4 2.0 collective-permute-start.9
  580.4 2.3 collective-permute-start.8
  582.7 1.5 collective-permute-done.9
  584.2 8.0 %collective-permute-done.8 = f32[3,1,64,256]{3,0,2,1:T(4,128)S(1)} collective-permute-done((f32[3,1,64,256]{3,0,2,1:T(4,128)S(1)}, f32[3,1,64,256]{3,0,2,1:T(4,128)S(1)}, u32[]{:S(2)}, u32[]{:S(2)}) %collective-permute-start.8) | collective-permute-done | bytes 196640 | tf_op jit(solution)/shard_map/ppermute | solution.py:15
  592.5 0.5 fusion.194
  593.2 1.3 fusion.85
  594.5 2.0 collective-permute-start.11
  596.5 2.3 collective-permute-start.10
  598.9 1.5 collective-permute-done.11
  600.4 8.0 %collective-permute-done.10 = f32[3,1,64,256]{3,0,2,1:T(4,128)S(1)} collective-permute-done((f32[3,1,64,256]{3,0,2,1:T(4,128)S(1)}, f32[3,1,64,256]{3,0,2,1:T(4,128)S(1)}, u32[]{:S(2)}, u32[]{:S(2)}) %collective-permute-start.10) | collective-permute-done | bytes 196640 | tf_op jit(solution)/shard_map/ppermute | solution.py:15
  609.4 1.3 convolution_bitcast_fusion
  610.7 0.7 copy.28
  (49 shorter events, 6.7 us)
Async XLA Ops:
  6.5 2.5 copy-start.4
  6.5 2.6 copy-start.5
  9.1 0.7 copy-start.1
  23.5 12.8 %copy-start.3 = (s32[65]{0:T(128)S(1)}, s32[65]{0:T(128)}, u32[]{:S(2)}) copy-start(s32[65]{0:T(128)} %param.10) | copy-start | bytes 784
  23.5 43.1 %all-to-all-start = ((f32[3,64,4,1,384]{4,2,3,0,1:T(4,128)}), f32[3,64,4,1,384]{4,2,3,0,1:T(4,128)S(1)}, u32[]{:S(2)}, u32[]{:S(2)}) async-start(f32[3,64,4,1,384]{4,2,3,0,1:T(4,128)} %copy.24), calls=%async_computation | async-start | bytes 2359296 | tf_op jit(solution)/shard_map/all_to_all | solution.py:80
  36.2 410.3 %reduce-scatter.2.cloned.1.call-start = ((), (), s32[]{:S(2)}) async-start(), calls=%async_computation.2 | async-start | bytes 62914560 | tf_op jit(solution)/shard_map/reduce_scatter | solution.py:81
  89.8 0.7 copy-start.2
  89.8 0.9 copy-start
  511.0 8.3 %collective-permute-start.1 = (f32[3,1,64,256]{3,0,2,1:T(4,128)S(1)}, f32[3,1,64,256]{3,0,2,1:T(4,128)S(1)}, u32[]{:S(2)}, u32[]{:S(2)}) collective-permute-start(f32[3,1,64,256]{3,0,2,1:T(4,128)S(1)} %broadcast_select_fusion), channel_id=1, source_target_pairs={{1,0},{2,1},{3,2},{4,3},{5,4},{6,5},{7,6},{8,7},{9,8},{10,9},{11,1... | collective-permute-start | bytes 589832 | tf_op jit(solution)/shard_map/ppermute | solution.py:18
  515.4 11.9 %collective-permute-start = (f32[3,1,64,256]{3,0,2,1:T(4,128)S(1)}, f32[3,1,64,256]{3,0,2,1:T(4,128)S(1)}, u32[]{:S(2)}, u32[]{:S(2)}) collective-permute-start(f32[3,1,64,256]{3,0,2,1:T(4,128)S(1)} %broadcast_select_fusion), channel_id=1, source_target_pairs={{0,1},{1,2},{2,3},{3,4},{4,5},{5,6},{6,7},{7,8},{8,9},{9,10},{10,1... | collective-permute-start | bytes 589832 | tf_op jit(solution)/shard_map/ppermute | solution.py:15
  528.0 0.7 copy-start.6
  530.0 5.8 collective-permute-start.3
  531.9 11.9 %collective-permute-start.2 = (f32[3,1,64,256]{3,0,2,1:T(4,128)S(1)}, f32[3,1,64,256]{3,0,2,1:T(4,128)S(1)}, u32[]{:S(2)}, u32[]{:S(2)}) collective-permute-start(f32[3,1,64,256]{3,0,2,1:T(4,128)S(1)} %bitcast.144), channel_id=1, source_target_pairs={{0,1},{1,2},{2,3},{3,4},{4,5},{5,6},{6,7},{7,8},{8,9},{9,10},{10,1... | collective-permute-start | bytes 589832 | tf_op jit(solution)/shard_map/ppermute | solution.py:15
  546.0 5.9 collective-permute-start.5
  548.0 11.9 %collective-permute-start.4 = (f32[3,1,64,256]{3,0,2,1:T(4,128)S(1)}, f32[3,1,64,256]{3,0,2,1:T(4,128)S(1)}, u32[]{:S(2)}, u32[]{:S(2)}) collective-permute-start(f32[3,1,64,256]{3,0,2,1:T(4,128)S(1)} %bitcast.147), channel_id=1, source_target_pairs={{0,1},{1,2},{2,3},{3,4},{4,5},{5,6},{6,7},{7,8},{8,9},{9,10},{10,1... | collective-permute-start | bytes 589832 | tf_op jit(solution)/shard_map/ppermute | solution.py:15
  562.2 5.9 collective-permute-start.7
  564.2 11.9 %collective-permute-start.6 = (f32[3,1,64,256]{3,0,2,1:T(4,128)S(1)}, f32[3,1,64,256]{3,0,2,1:T(4,128)S(1)}, u32[]{:S(2)}, u32[]{:S(2)}) collective-permute-start(f32[3,1,64,256]{3,0,2,1:T(4,128)S(1)} %bitcast.150), channel_id=1, source_target_pairs={{0,1},{1,2},{2,3},{3,4},{4,5},{5,6},{6,7},{7,8},{8,9},{9,10},{10,1... | collective-permute-start | bytes 589832 | tf_op jit(solution)/shard_map/ppermute | solution.py:15
  578.4 5.9 collective-permute-start.9
  580.4 11.9 %collective-permute-start.8 = (f32[3,1,64,256]{3,0,2,1:T(4,128)S(1)}, f32[3,1,64,256]{3,0,2,1:T(4,128)S(1)}, u32[]{:S(2)}, u32[]{:S(2)}) collective-permute-start(f32[3,1,64,256]{3,0,2,1:T(4,128)S(1)} %bitcast.153), channel_id=1, source_target_pairs={{0,1},{1,2},{2,3},{3,4},{4,5},{5,6},{6,7},{7,8},{8,9},{9,10},{10,1... | collective-permute-start | bytes 589832 | tf_op jit(solution)/shard_map/ppermute | solution.py:15
  594.5 5.9 collective-permute-start.11
  596.5 11.9 %collective-permute-start.10 = (f32[3,1,64,256]{3,0,2,1:T(4,128)S(1)}, f32[3,1,64,256]{3,0,2,1:T(4,128)S(1)}, u32[]{:S(2)}, u32[]{:S(2)}) collective-permute-start(f32[3,1,64,256]{3,0,2,1:T(4,128)S(1)} %bitcast.141), channel_id=1, source_target_pairs={{0,1},{1,2},{2,3},{3,4},{4,5},{5,6},{6,7},{7,8},{8,9},{9,10},{10,1... | collective-permute-start | bytes 589832 | tf_op jit(solution)/shard_map/ppermute | solution.py:15
Sparse Core Ops, SparseCore 0:
  89.9 356.5 reduce-scatter.1
where the time goes:
time: 625 us; the launch traced here: 618 us
  waiting for transfers between devices  442 us (71%)
  local copies, waits for them, and re-layouts  103 us (16%)
  starting transfers between devices  40.9 us (7%)
  between operations  13.8 us (2%)
  matrix products  8.09 us (1%)
  loops' own time  7.5 us (1%)
    reduce_scatter x1, waiting for transfers between devices, shards(): summed = lax.psum_scatter(moved, 'par', scatter_dimension=2, tiled=True)  356 us
    gather x2, local copies, waits for them, and re-layouts, shards(): jnp.take(padded_slots, slot_index, axis=2)  64.4 us
    ppermute x6, waiting for transfers between devices, extended(): lax.ppermute(lax.slice_in_dim(block, block.shape[dim] - width, None, axis...  48.2 us
    all_to_all x1, waiting for transfers between devices, shards(): lax.all_to_all(blocks, 'cols', split_axis=1, concat_axis=4, tiled=True)  29 us
    all_to_all x1, local copies, waits for them, and re-layouts, shards(): lax.all_to_all(blocks, 'cols', split_axis=1, concat_axis=4, tiled=True)  23.2 us
    ppermute x6, starting transfers between devices, extended(): lax.ppermute(lax.slice_in_dim(block, 0, width, axis=dim), axis, backward)  14.3 us
    ppermute x6, starting transfers between devices, extended(): lax.ppermute(lax.slice_in_dim(block, block.shape[dim] - width, None, axis...  13.8 us
    all_to_all x1, starting transfers between devices, shards(): lax.all_to_all(blocks, 'cols', split_axis=1, concat_axis=4, tiled=True)  12.7 us
  transfers between devices with their start and end apart: 14, of which 14 were waited for; matrix products, arithmetic and copies ran while one was open for 0% of the time, Pallas kernels for 0%

commit v1 on v0

v1 whole, which is shorter than its diff:
```python
import functools

import jax
import jax.numpy as jnp
from jax import lax
from jax.experimental import pallas as pl
from jax.experimental.pallas import tpu as pltpu
from jax.sharding import PartitionSpec as P

CAP = 384
PASSES = 6
F32 = jnp.float32
VMEM = pl.BlockSpec(memory_space=pltpu.VMEM)
SMEM = pl.BlockSpec(memory_space=pltpu.SMEM)


def layer_of(cols, par):
    plane, y_lo, x = cols // 8, (cols // 4) % 2, cols % 4
    y_hi, core = par // 2, par % 2
    place = 4 * (2 * y_hi + y_lo) + x + y_lo * (3 - 2 * x)
    place = place + (plane % 2) * (15 - 2 * place)
    return 32 * plane + 2 * place + core


def holder_of(layer):
    plane, rest = layer // 32, layer % 32
    place, core = rest // 2, rest % 2
    place = place + (plane % 2) * (15 - 2 * place)
    y, x = place // 4, place % 4
    y_lo = y % 2
    x = x + y_lo * (3 - 2 * x)
    return 8 * plane + 4 * y_lo + x, 2 * (y // 2) + core


def to(cols, par):
    return dict(device_id={"cols": cols, "par": par}, device_id_type=pl.DeviceIdType.MESH)


def contribution_kernel(picks, rmo, sens, out):
    tiles, rays = rmo.shape
    ray = lax.broadcasted_iota(jnp.int32, (1, rays), 1)
    for t in range(tiles):
        weight = jnp.where(ray < picks[t], rmo[t : t + 1, :].astype(F32), 0.0)
        total = jnp.zeros(out.shape[1:], F32)
        for r in range(rays):
            total += weight[:, r : r + 1][None] * sens[t, r].astype(F32)
        out[t] = total


def share_kernel(anchor, mine, tiles, anchors, mine_anchor, sends, recvs, anchor_sends, anchor_recvs):
    cols, par = lax.axis_index("cols"), lax.axis_index("par")
    peers = [(par + step) % 4 for step in (1, 2, 3)]
    barrier = pltpu.get_barrier_semaphore()
    for peer in peers:
        pl.semaphore_signal(barrier, inc=1, **to(cols, peer))
    row = lax.broadcasted_iota(jnp.int32, (8, 128), 0)
    lane = lax.broadcasted_iota(jnp.int32, (8, 128), 1)
    table = jnp.zeros((8, 128), jnp.int32)
    for t in range(2):
        for k in range(2):
            table = jnp.where((row == t) & (lane == k), anchor[t, k], table)
    mine_anchor[...] = table
    anchors[par] = table
    tiles[par] = mine[...]
    pl.semaphore_wait(barrier, 3)
    copies = []
    for step, peer in enumerate(peers):
        copies.append(
            pltpu.make_async_remote_copy(
                mine_anchor, anchors.at[par], anchor_sends.at[step], anchor_recvs.at[step], **to(cols, peer)
            )
        )
        copies.append(
            pltpu.make_async_remote_copy(mine, tiles.at[par], sends.at[step], recvs.at[step], **to(cols, peer))
        )
    for copy in copies:
        copy.start()
    for copy in copies:
        copy.wait()


def place_kernel(tiles, anchors, rows, placed):
    par = lax.axis_index("par")
    count = rows.shape[0] - 1

    def clear(i, carry):
        rows[i] = jnp.zeros(rows.shape[1:], F32)
        return carry

    lax.fori_loop(0, count + 1, clear, 0)
    for q in range(4):
        table = anchors[q]
        for t in range(2):
            first, shift = table[t, 0], table[t, 1]
            tile = tiles[q, t].reshape(48, 128)
            tile = jnp.concatenate([tile, jnp.zeros((48, CAP - 128), F32)], axis=1)
            tile = pltpu.roll(tile, shift, 1)
            for j in range(CAP // 128):
                placed[j] = tile[:, 128 * j : 128 * (j + 1)]
            for k in range(16):
                cols, owner = holder_of(first + k)
                spot = jnp.where(owner == par, cols, count)
                parts = [placed[j, pl.ds(k, 3, stride=16), :] for j in range(CAP // 128)]
                rows[spot] += jnp.concatenate(parts, axis=1)


def spread_kernel(rows, dip, spread, dip_out, send, recv, dip_send, dip_recv):
    cols, par = lax.axis_index("cols"), lax.axis_index("par")
    count = spread.shape[0]
    layer = layer_of(cols, par)
    mine = 4 * cols + par
    source_cols, source_par = layer // 4, layer % 4
    target_cols, target_par = holder_of(mine)
    same = (target_cols == cols) & (target_par == par)
    barrier = pltpu.get_barrier_semaphore()

    def greet(step, carry):
        pl.semaphore_signal(barrier, inc=1, **to((cols + step) % count, par))
        return carry

    lax.fori_loop(1, count, greet, 0)

    @pl.when(jnp.logical_not(same))
    def _():
        pl.semaphore_signal(barrier, inc=1, **to(source_cols, source_par))

    spread[cols] = rows[cols]
    pl.semaphore_wait(barrier, jnp.where(same, count - 1, count))

    def put(step, carry):
        peer = (cols + step) % count
        pltpu.make_async_remote_copy(rows.at[peer], spread.at[cols], send, recv, **to(peer, par)).start()
        return carry

    lax.fori_loop(1, count, put, 0)

    dip_copy = pltpu.make_async_remote_copy(dip, dip_out, dip_send, dip_recv, **to(target_cols, target_par))

    @pl.when(jnp.logical_not(same))
    def _():
        dip_copy.start()
        dip_copy.wait()

    @pl.when(same)
    def _():
        dip_out[...] = dip[...]

    others = spread.at[pl.ds(0, count - 1)]
    pltpu.make_async_copy(others, others, recv).wait()
    pltpu.make_async_copy(others, others, send).wait()


def lateral_kernel(bounds, spread, field, stage):
    count = spread.shape[0]
    params, rows_x, rows_y = field.shape

    def clear(i, carry):
        stage[:, pl.ds(pl.multiple_of(8 * i, 8), 8), :] = jnp.zeros((rows_y // 128, 8, 128), F32)
        return carry

    lax.fori_loop(0, stage.shape[1] // 8, clear, 0)

    def add(c, carry):
        start = bounds[c]
        row, shift = start // rows_y, start % rows_y
        part = jnp.concatenate([spread[c], jnp.zeros((8 - params, CAP), F32)], axis=0)
        part = jnp.concatenate([part, jnp.zeros((8, 3 * rows_y - CAP), F32)], axis=1)
        part = pltpu.roll(part, shift, 1)
        for k in range(3):
            spot = pl.ds(pl.multiple_of(8 * (row + k), 8), 8)
            for j in range(rows_y // 128):
                lane = k * rows_y + j * 128
                stage[j, spot, :] += part[:, lane : lane + 128]
        return carry

    lax.fori_loop(0, count, add, 0)
    for p in range(params):
        for k in range(rows_y // 128):
            field[p, :, pl.ds(k * 128, 128)] = stage[k, pl.ds(p, rows_x, stride=8), :]


def smooth_kernel(
    strength, couple, start, dip, out, fields, below, above, sends_up, recvs_up, sends_down, recvs_down, out_send, out_recv
):
    cols, par = lax.axis_index("cols"), lax.axis_index("par")
    params, rows_x, rows_y = start.shape
    layer = layer_of(cols, par)
    layers = 4 * lax.axis_size("cols")
    has_down, has_up = layer > 0, layer < layers - 1
    down_device = to(*holder_of(jnp.maximum(layer - 1, 0)))
    up_device = to(*holder_of(jnp.minimum(layer + 1, layers - 1)))
    target_cols, target_par = layer // 4, layer % 4
    source_cols, source_par = holder_of(4 * cols + par)
    same = (target_cols == cols) & (target_par == par)

    barrier = pltpu.get_barrier_semaphore()

    @pl.when(has_down)
    def _():
        pl.semaphore_signal(barrier, inc=1, **down_device)

    @pl.when(has_up)
    def _():
        pl.semaphore_signal(barrier, inc=1, **up_device)

    @pl.when(jnp.logical_not(same))
    def _():
        pl.semaphore_signal(barrier, inc=1, **to(source_cols, source_par))

    @pl.when(jnp.logical_not(has_down))
    def _():
        below[...] = jnp.zeros_like(below)

    @pl.when(jnp.logical_not(has_up))
    def _():
        above[...] = jnp.zeros_like(above)

    scale = []
    for p in range(params):
        row_sum = jnp.full((8, 128), couple[p, 0] + couple[p, 1] + couple[p, 2], F32)
        scale.append([(jnp.full((8, 128), couple[p, q], F32) / row_sum)[0, 0] for q in range(params)])

    tilt_x = dip[...] // 3 - 1
    tilt_y = dip[...] % 3 - 1
    at_x = lax.broadcasted_iota(jnp.int32, (rows_x, rows_y), 0)
    at_y = lax.broadcasted_iota(jnp.int32, (rows_x, rows_y), 1)

    pl.semaphore_wait(barrier, jnp.where(has_down, 1, 0) + jnp.where(has_up, 1, 0) + jnp.where(same, 0, 1))

    def pick(tilt, low, mid, high):
        return jnp.where(tilt < 0, low, jnp.where(tilt > 0, high, mid))

    for step in range(PASSES):
        slot = step % 2
        field = start if step == 0 else fields.at[slot]
        upward = pltpu.make_async_remote_copy(field, below.at[slot], sends_up.at[slot], recvs_up.at[slot], **up_device)
        downward = pltpu.make_async_remote_copy(field, above.at[slot], sends_down.at[slot], recvs_down.at[slot], **down_device)

        @pl.when(has_up)
        def _():
            upward.start()

        @pl.when(has_down)
        def _():
            downward.start()

        @pl.when(has_up)
        def _():
            upward.wait_send()
            downward.wait_recv()

        @pl.when(has_down)
        def _():
            downward.wait_send()
            upward.wait_recv()

        smooth = []
        for p in range(params):
            low, mid, high = below[slot, p], field[p], above[slot, p]
            rolled = lambda v, by, axis: pltpu.roll(v, by % v.shape[axis], axis)
            east = [rolled(v, -1, 0) for v in (low, mid, high)]
            west = [rolled(v, 1, 0) for v in (low, mid, high)]
            north = [rolled(v, -1, 1) for v in (low, mid, high)]
            south = [rolled(v, 1, 1) for v in (low, mid, high)]
            laplace = jnp.where(at_x < rows_x - 1, pick(tilt_x, *east), 0.0)
            laplace += jnp.where(at_x > 0, pick(tilt_x, *west[::-1]), 0.0)
            laplace += jnp.where(at_y < rows_y - 1, pick(tilt_y, *north), 0.0)
            laplace += jnp.where(at_y > 0, pick(tilt_y, *south[::-1]), 0.0)
            smooth.append(mid + strength[p] * (laplace - 4.0 * mid))
        for p in range(params):
            value = scale[p][0] * smooth[0] + scale[p][1] * smooth[1] + scale[p][2] * smooth[2]
            fields[1 - slot, p] = value

    last = fields.at[PASSES % 2]
    final = pltpu.make_async_remote_copy(last, out, out_send, out_recv, **to(target_cols, target_par))

    @pl.when(jnp.logical_not(same))
    def _():
        final.start()
        final.wait()

    @pl.when(same)
    def _():
        out[...] = last[...]


def shards(tile_bounds, tile_anchor, tile_picks, rmo_picks, sensitivity, dip_class, strength, couple):
    tile_count, ray_count, params, tile_z, tile_c = sensitivity.shape
    count = lax.axis_size("cols")
    _, rows_x, rows_y = dip_class.shape
    shape = jax.ShapeDtypeStruct
    dma = pltpu.SemaphoreType.DMA
    remote = lambda number: pltpu.CompilerParams(collective_id=number, has_side_effects=True)

    mine = pl.pallas_call(
        contribution_kernel,
        out_shape=shape((tile_count, params, tile_z, tile_c), F32),
        in_specs=[SMEM, VMEM, VMEM],
        out_specs=VMEM,
        name="contribution",
    )(tile_picks, rmo_picks, sensitivity)
    tiles, anchors = pl.pallas_call(
        share_kernel,
        out_shape=(shape((4, tile_count, params, tile_z, tile_c), F32), shape((4, 8, 128), jnp.int32)),
        in_specs=[SMEM, VMEM],
        out_specs=(VMEM, VMEM),
        scratch_shapes=[pltpu.VMEM((8, 128), jnp.int32), dma((3,)), dma((3,)), dma((3,)), dma((3,))],
        compiler_params=remote(0),
        name="share",
    )(tile_anchor, mine)
    rows = pl.pallas_call(
        place_kernel,
        out_shape=shape((count + 1, params, CAP), F32),
        in_specs=[VMEM, VMEM],
        out_specs=VMEM,
        scratch_shapes=[pltpu.VMEM((CAP // 128, params * tile_z, 128), F32)],
        name="place",
    )(tiles, anchors)
    spread, dip = pl.pallas_call(
        spread_kernel,
        out_shape=(shape((count, params, CAP), F32), shape((rows_x, rows_y), jnp.int32)),
        in_specs=[VMEM, VMEM],
        out_specs=(VMEM, VMEM),
        scratch_shapes=[dma, dma, dma, dma],
        compiler_params=remote(1),
        name="spread",
    )(rows, dip_class.reshape(rows_x, rows_y))
    start = pl.pallas_call(
        lateral_kernel,
        out_shape=shape((params, rows_x, rows_y), F32),
        in_specs=[SMEM, VMEM],
        out_specs=VMEM,
        scratch_shapes=[pltpu.VMEM((rows_y // 128, (rows_x + 3) * 8, 128), F32)],
        name="lateral",
    )(tile_bounds, spread)
    buffer = pltpu.VMEM((2, params, rows_x, rows_y), F32)
    field = pl.pallas_call(
        smooth_kernel,
        out_shape=shape((params, rows_x, rows_y), F32),
        in_specs=[SMEM, SMEM, VMEM, VMEM],
        out_specs=VMEM,
        scratch_shapes=[buffer, buffer, buffer, dma((2,)), dma((2,)), dma((2,)), dma((2,)), dma, dma],
        compiler_params=remote(2),
        name="smooth",
    )(strength, couple, start, dip)
    return field.reshape(params, 1, rows_x, rows_y)


def solution(mesh):
    return jax.shard_map(
        shards,
        mesh=mesh,
        in_specs=(
            P(),
            P(("cols", "par"), None),
            P(("cols", "par")),
            P(("cols", "par"), None),
            P(("cols", "par"), None, None, None, None),
            P(("cols", "par"), None, None),
            P(),
            P(),
        ),
        out_specs=P(None, ("cols", "par"), None, None),
        check_vma=False,
    )
```

time: 625 us -> 92.4 us (0.15)
  waiting for transfers between devices: 442 us -> 0 us
  local copies, waits for them, and re-layouts: 103 us -> 1.62 us
  Pallas kernels: 0 us -> 89.7 us
  starting transfers between devices: 40.9 us -> 0 us
  between operations: 13.8 us -> 0.03 us
  matrix products: 8.09 us -> 0 us
  loops' own time: 7.5 us -> 0 us
    reduce_scatter x1 -> x0, waiting for transfers between devices: 356 us -> none  [shards(): summed = lax.psum_scatter(moved, 'par', scatter_dimension=2, tiled=True)]
    pallas_call x0 -> x6, Pallas kernels: none -> 89.7 us  [the longest x1 43.8 us: shards(): pl.pallas_call(smooth_kernel, out_shape=shape((params, rows_x, rows_y), F...]
    gather x2 -> x0, local copies, waits for them, and re-layouts: 64.4 us -> none  [shards(): jnp.take(padded_slots, slot_index, axis=2)]
    ppermute x12 -> x0, waiting for transfers between devices: 57.6 us -> none  [the longest x6 48.2 us: extended(): lax.ppermute(lax.slice_in_dim(block, block.shape[dim] - width, None, axis...]
    all_to_all x1 -> x0, waiting for transfers between devices: 29 us -> none  [shards(): lax.all_to_all(blocks, 'cols', split_axis=1, concat_axis=4, tiled=True)]
    ppermute x12 -> x0, starting transfers between devices: 28.1 us -> none  [the longest x6 14.3 us: extended(): lax.ppermute(lax.slice_in_dim(block, 0, width, axis=dim), axis, backward)]
    all_to_all x1 -> x0, local copies, waits for them, and re-layouts: 23.2 us -> none  [shards(): lax.all_to_all(blocks, 'cols', split_axis=1, concat_axis=4, tiled=True)]
    all_to_all x1 -> x0, starting transfers between devices: 12.7 us -> none  [shards(): lax.all_to_all(blocks, 'cols', split_axis=1, concat_axis=4, tiled=True)]
  transfers between devices with their start and end apart: 14 -> 0, of which waited for: 14 -> 0; matrix products, arithmetic and copies ran while one was open for 0% -> 0% of each run, Pallas kernels for 0% -> 0%
where the time goes in v1:
time: 92.4 us; the launch traced here: 91.3 us
  Pallas kernels  89.7 us (97%)
  local copies, waits for them, and re-layouts  1.62 us (2%)
    pallas_call x1, Pallas kernels, shards(): pl.pallas_call(smooth_kernel, out_shape=shape((params, rows_x, rows_y), F...  43.8 us
    pallas_call x1, Pallas kernels, shards(): pl.pallas_call(spread_kernel, out_shape=(shape((count, params, CAP), F32)...  22.7 us
    pallas_call x1, Pallas kernels, shards(): pl.pallas_call(share_kernel, out_shape=(shape((4, tile_count, params, til...  7.83 us
    pallas_call x1, Pallas kernels, shards(): pl.pallas_call(lateral_kernel, out_shape=shape((params, rows_x, rows_y),...  7.26 us
    pallas_call x1, Pallas kernels, shards(): pl.pallas_call(place_kernel, out_shape=shape((count + 1, params, CAP), F3...  5.67 us
    pallas_call x1, Pallas kernels, shards(): pl.pallas_call(contribution_kernel, out_shape=shape((tile_count, params,...  2.49 us

profile of v1, /device:TPU:32, one launch (start us, length us, event | category | flops | bytes accessed | tf_op | source)
XLA Modules:
  0.0 91.3 jit_solution(14539285319768359215)
XLA Ops:
  0.0 2.5 %contribution.1.mine = f32[2,3,16,128]{3,2,1,0:T(8,128)} custom-call(s32[2]{0:T(128)} %picks.1, bf16[2,64]{1,0:T(2,128)(2,1)} %rmo.1, bf16[2,64,3,16,128]{4,3,2,1,0:T(8,128)(2,1)} %sens.1), custom_call_target="tpu_custom_call" | custom-call | tf_op jit(solution)/shard_map/contribution/pallas_call | solution.py:295
  2.5 7.8 %share.1 = (f32[4,2,3,16,128]{4,3,2,1,0:T(8,128)}, s32[4,8,128]{2,1,0:T(8,128)}) custom-call(s32[2,2]{1,0:T(2,128)} %anchor.1, f32[2,3,16,128]{3,2,1,0:T(8,128)} %contribution.1.mine), custom_call_target="tpu_custom_call" | custom-call | tf_op jit(solution)/shard_map/share/pallas_call | solution.py:302
  10.3 5.7 %place.1.rows = f32[65,3,384]{2,1,0:T(4,128)} custom-call(f32[4,2,3,16,128]{4,3,2,1,0:T(8,128)} %get-tuple-element.9.tiles, s32[4,8,128]{2,1,0:T(8,128)} %get-tuple-element.10.anchors), custom_call_target="tpu_custom_call" | custom-call | tf_op jit(solution)/shard_map/place/pallas_call | solution.py:311
  16.0 22.7 %spread.1 = (f32[64,3,384]{2,1,0:T(4,128)}, s32[64,256]{1,0:T(8,128)}) custom-call(f32[65,3,384]{2,1,0:T(4,128)} %place.1.rows, s32[64,256]{1,0:T(8,128)} %bitcast.5), custom_call_target="tpu_custom_call" | custom-call | tf_op jit(solution)/shard_map/spread/pallas_call | solution.py:319
  38.7 7.3 %lateral.1.start = f32[3,64,256]{2,1,0:T(8,128)} custom-call(s32[65]{0:T(128)} %bounds.1, f32[64,3,384]{2,1,0:T(4,128)} %get-tuple-element.11.spread), custom_call_target="tpu_custom_call" | custom-call | tf_op jit(solution)/shard_map/lateral/pallas_call | solution.py:328
  45.9 43.8 %smooth.1 = f32[3,64,256]{2,1,0:T(8,128)} custom-call(f32[3]{0:T(128)} %strength.1, f32[3,3]{1,0:T(4,128)} %couple.1, f32[3,64,256]{2,1,0:T(8,128)} %lateral.1.start, s32[64,256]{1,0:T(8,128)} %get-tuple-element.12.dip), custom_call_target="tpu_custom_call" | custom-call | tf_op jit(solution)/shard_map/smooth/pallas_call | solution.py:337
  89.7 1.6 %copy.11 = f32[3,1,64,256]{3,2,1,0:T(8,128)} copy(f32[3,1,64,256]{3,2,1,0:T(8,128)} %bitcast.4) | data formatting | bytes 393216

commit v2 on v0

v2 whole, which is shorter than its diff:
```python
import jax
import jax.numpy as jnp
from jax import lax
from jax.experimental import pallas as pl
from jax.experimental.pallas import tpu as pltpu
from jax.sharding import PartitionSpec as P

CAP = 384
PASSES = 6
CHUNK = 8
F32 = jnp.float32
VMEM = pl.BlockSpec(memory_space=pltpu.VMEM)
SMEM = pl.BlockSpec(memory_space=pltpu.SMEM)


def layer_of(cols, par):
    plane, y_lo, x = cols // 8, (cols // 4) % 2, cols % 4
    y_hi, core = par // 2, par % 2
    place = 4 * (2 * y_hi + y_lo) + x + y_lo * (3 - 2 * x)
    place = place + (plane % 2) * (15 - 2 * place)
    return 32 * plane + 2 * place + core


def holder_of(layer):
    plane, rest = layer // 32, layer % 32
    place, core = rest // 2, rest % 2
    place = place + (plane % 2) * (15 - 2 * place)
    y, x = place // 4, place % 4
    y_lo = y % 2
    x = x + y_lo * (3 - 2 * x)
    return 8 * plane + 4 * y_lo + x, 2 * (y // 2) + core


def to(cols, par):
    return dict(device_id={"cols": cols, "par": par}, device_id_type=pl.DeviceIdType.MESH)


def step_kernel(
    bounds, anchor, picks, strength, couple, rmo, dip_in, sens_in, out,
    sens, tiles, placed, rows, spread, dip, table, rolled, stage, fields, below, above,
    sens_sem, share_send, share_recv, spread_send, spread_recv, dip_send, dip_recv,
    sends_up, recvs_up, sends_down, recvs_down, out_send, out_recv,
):
    cols, par = lax.axis_index("cols"), lax.axis_index("par")
    count = spread.shape[0]
    params, rows_x, rows_y = out.shape
    chunks = rows_x // CHUNK
    layer, layers = layer_of(cols, par), 4 * count
    has_down, has_up = layer > 0, layer < layers - 1
    down_device = to(*holder_of(jnp.maximum(layer - 1, 0)))
    up_device = to(*holder_of(jnp.minimum(layer + 1, layers - 1)))
    target_cols, target_par = layer // 4, layer % 4
    holder_cols, holder_par = holder_of(4 * cols + par)
    same = (target_cols == cols) & (target_par == par)
    other = jnp.logical_not(same)

    load = pltpu.make_async_copy(sens_in, sens, sens_sem)
    load.start()
    barrier = pltpu.get_barrier_semaphore()

    def greet(step, carry):
        pl.semaphore_signal(barrier, inc=1, **to((cols + step) % count, par))
        return carry

    lax.fori_loop(1, count, greet, 0)
    for step in (1, 2, 3):
        pl.semaphore_signal(barrier, inc=1, **to(cols, (par + step) % 4))

    @pl.when(has_down)
    def _():
        pl.semaphore_signal(barrier, inc=1, **down_device)

    @pl.when(has_up)
    def _():
        pl.semaphore_signal(barrier, inc=1, **up_device)

    @pl.when(other)
    def _():
        pl.semaphore_signal(barrier, inc=1, **to(target_cols, target_par))
        pl.semaphore_signal(barrier, inc=1, **to(holder_cols, holder_par))

    def find(line, seen):
        hit = jnp.where(bounds[seen] // 128 == line, 1, 0)
        table[line + 3] = jnp.where(hit == 1, seen, count)
        return seen + hit

    for k in range(3):
        table[k] = count
    lax.fori_loop(0, table.shape[0] - 3, find, 0)

    @pl.when(jnp.logical_not(has_down))
    def _():
        below[...] = jnp.zeros_like(below)

    @pl.when(jnp.logical_not(has_up))
    def _():
        above[...] = jnp.zeros_like(above)

    edge = jnp.zeros((2, params, 8, rows_y), F32)
    for ref in (fields, below, above):
        ref[:, :, pl.ds(0, 8), :] = edge
        ref[:, :, pl.ds(rows_x + 8, 8), :] = edge
    rolled[pl.ds(4 * count, 4)] = jnp.zeros((4, 8, 128), F32)

    scale = []
    for p in range(params):
        row_sum = jnp.full((8, 128), couple[p, 0] + couple[p, 1] + couple[p, 2], F32)
        scale.append([(jnp.full((8, 128), couple[p, q], F32) / row_sum)[0, 0] for q in range(params)])

    ray = lax.broadcasted_iota(jnp.int32, (1, rmo.shape[1]), 1)
    weights = [jnp.where(ray < picks[t], rmo[t : t + 1, :].astype(F32), 0.0) for t in range(2)]
    lane = lax.broadcasted_iota(jnp.int32, (48, 128), 1)
    row = lax.broadcasted_iota(jnp.int32, (8, 128), 0)
    load.wait()
    for t in range(2):
        total = jnp.zeros((params, 16, 128), F32)
        for r in range(rmo.shape[1]):
            total += weights[t][:, r : r + 1][None] * sens[t, r].astype(F32)
        tiles[0, pl.ds(48 * t, 48), :] = total.reshape(48, 128)
    facts = jnp.zeros((8, 128), F32)
    for k, value in enumerate((anchor[0, 0], anchor[1, 0], anchor[0, 1], anchor[1, 1])):
        facts = jnp.where(row == k, value.astype(F32), facts)
    tiles[0, pl.ds(96, 8), :] = facts

    remote_pairs = jnp.where(same, 0, 2)
    pl.semaphore_wait(barrier, count + 2 + remote_pairs + jnp.where(has_down, 1, 0) + jnp.where(has_up, 1, 0))

    shares = [
        pltpu.make_async_remote_copy(
            tiles.at[0], tiles.at[step], share_send.at[step - 1], share_recv.at[step - 1], **to(cols, (par + step) % 4)
        )
        for step in (1, 2, 3)
    ]
    for share in (shares[1], shares[2], shares[0]):
        share.start()
    dip_copy = pltpu.make_async_remote_copy(dip_in, dip, dip_send, dip_recv, **to(holder_cols, holder_par))

    @pl.when(other)
    def _():
        dip_copy.start()

    @pl.when(same)
    def _():
        dip[...] = dip_in[...]

    place = lax.broadcasted_iota(jnp.int32, (4 * count, 384), 0)
    item = lax.broadcasted_iota(jnp.int32, (4 * count, 384), 1)
    wanted = jnp.where(place % 4 == (item // 16) % 3, layer_of(place // 4, par) - item % 16, -1).astype(F32)
    item = lax.broadcasted_iota(jnp.int32, (1, 384), 1) // 48
    first = jnp.zeros((1, 384), F32)

    for slot in (0, 1, 2, 3):
        if slot:
            shares[slot - 1].wait()
        facts = tiles[slot, pl.ds(96, 8), :]
        wide = jnp.concatenate([facts] * 3, axis=1)
        for t in range(2):
            first = jnp.where(item == 2 * slot + t, wide[t : t + 1], first)
            shift = facts[2 + t, 0].astype(jnp.int32)
            fine, coarse = shift % 128, shift // 128
            tile = pltpu.roll(tiles[slot, pl.ds(48 * t, 48), :], fine, 1)
            keep = jnp.where(lane >= fine, tile, 0.0)
            wrap = tile - keep
            spot = pl.ds(96 * slot + 48 * t, 48)
            placed[spot, pl.ds(0, 128)] = jnp.where(coarse == 0, keep, 0.0)
            placed[spot, pl.ds(128, 128)] = jnp.where(coarse == 0, wrap, jnp.where(coarse == 1, keep, 0.0))
            placed[spot, pl.ds(256, 128)] = jnp.where(coarse == 2, keep, jnp.where(coarse == 1, wrap, 0.0))

    match = jnp.where(wanted == first, 1.0, 0.0).astype(jnp.bfloat16)
    value = placed[...]
    total = jnp.zeros((4 * count, CAP), F32)
    for _ in range(3):
        piece = value.astype(jnp.bfloat16)
        total += jnp.dot(match, piece, preferred_element_type=F32)
        value = value - piece.astype(F32)
    for c in range(count):
        rows[c] = total[4 * c : 4 * c + params]

    def put(i, carry):
        peer = (cols + (i + count // 2 - 1) % (count - 1) + 1) % count
        pltpu.make_async_remote_copy(rows.at[peer], spread.at[cols], spread_send, spread_recv, **to(peer, par)).start()
        return carry

    lax.fori_loop(0, count - 1, put, 0)
    spread[cols] = rows[cols]

    at_y = lax.broadcasted_iota(jnp.int32, (CHUNK, rows_y), 1)
    west_edge, east_edge = at_y == 0, at_y == rows_y - 1

    def chunk_of(c):
        return pl.ds(8 + CHUNK * c, CHUNK)

    def upward(slot, c):
        piece = (slot, slice(None), chunk_of(c))
        return pltpu.make_async_remote_copy(
            fields.at[piece], below.at[piece], sends_up.at[slot, c], recvs_up.at[slot, c], **up_device
        )

    def downward(slot, c):
        piece = (slot, slice(None), chunk_of(c))
        return pltpu.make_async_remote_copy(
            fields.at[piece], above.at[piece], sends_down.at[slot, c], recvs_down.at[slot, c], **down_device
        )

    def finish(c):
        return pltpu.make_async_remote_copy(
            fields.at[PASSES % 2, :, chunk_of(c)],
            out.at[:, pl.ds(CHUNK * c, CHUNK)],
            out_send,
            out_recv,
            **to(target_cols, target_par),
        )

    def send(slot, c):
        @pl.when(has_up)
        def _():
            upward(slot, c).start()

        @pl.when(has_down)
        def _():
            downward(slot, c).start()

    def receive(slot, c):
        @pl.when(has_down)
        def _():
            upward(slot, c).wait_recv()

        @pl.when(has_up)
        def _():
            downward(slot, c).wait_recv()

    def sent(slot, c):
        @pl.when(has_up)
        def _():
            upward(slot, c).wait_send()

        @pl.when(has_down)
        def _():
            downward(slot, c).wait_send()

    def pick(lower, higher, low, mid, high):
        return jnp.where(lower, low, jnp.where(higher, high, mid))

    others = spread.at[pl.ds(0, count - 1)]
    pltpu.make_async_copy(others, others, spread_recv).wait()

    lane = lax.broadcasted_iota(jnp.int32, (8, 128), 1)
    blank = jnp.zeros((8 - params, 128), F32)

    def turn(c, carry):
        fine = bounds[c] % 128
        before = jnp.zeros((8, 128), F32)
        for k in range(4):
            if k < 3:
                part = jnp.concatenate([spread[c, :, pl.ds(128 * k, 128)], blank], axis=0)
                part = pltpu.roll(part, fine, 1)
            else:
                part = jnp.zeros((8, 128), F32)
            rolled[4 * c + k] = jnp.where(lane >= fine, part, before)
            before = part
        return carry

    lax.fori_loop(0, count, turn, 0, unroll=4)
    for c in range(chunks):

        def gather(line, carry):
            total = rolled[4 * table[line + 3]]
            for k in range(1, 4):
                total += rolled[4 * table[line + 3 - k] + k]
            stage[pl.ds(pl.multiple_of(8 * line, 8), 8), :] = total
            return carry

        per_chunk = CHUNK * rows_y // 128
        lax.fori_loop(per_chunk * c, per_chunk * (c + 1), gather, 0, unroll=4)
        for p in range(params):
            for k in range(rows_y // 128):
                piece = stage[pl.ds(8 * per_chunk * c + 8 * k + p, CHUNK, stride=8 * rows_y // 128), :]
                fields[0, p, chunk_of(c), pl.ds(128 * k, 128)] = piece
        send(0, c)

    @pl.when(other)
    def _():
        dip_copy.wait()

    for step in range(PASSES):
        slot = step % 2
        for c in range(chunks):
            if c == 0:
                receive(slot, 0)
            if c + 1 < chunks:
                receive(slot, c + 1)
            if step > 0:
                sent(1 - slot, c)
            first = 8 + CHUNK * c
            kind = dip[pl.ds(CHUNK * c, CHUNK), :]
            across_low, across_high = kind < 3, kind >= 6
            along = kind - jnp.where(across_low, 0, jnp.where(across_high, 6, 3))
            along_low, along_high = along == 0, along == 2
            smooth = []
            for p in range(params):
                def rows(shift):
                    piece = (slot, p, pl.ds(first + shift, CHUNK))
                    return below[piece], fields[piece], above[piece]
                def rolled(values, by):
                    return [pltpu.roll(v, by % rows_y, 1) for v in values]
                here = rows(0)
                laplace = pick(across_low, across_high, *rows(1))
                laplace += pick(across_low, across_high, *rows(-1)[::-1])
                laplace += jnp.where(east_edge, 0.0, pick(along_low, along_high, *rolled(here, -1)))
                laplace += jnp.where(west_edge, 0.0, pick(along_low, along_high, *rolled(here, 1)[::-1]))
                smooth.append(here[1] + strength[p] * (laplace - 4.0 * here[1]))
            for p in range(params):
                value = scale[p][0] * smooth[0] + scale[p][1] * smooth[1] + scale[p][2] * smooth[2]
                fields[1 - slot, p, pl.ds(first, CHUNK), :] = value
                if step == PASSES - 1:
                    @pl.when(same)
                    def _():
                        out[p, pl.ds(CHUNK * c, CHUNK), :] = value
            if step < PASSES - 1:
                send(1 - slot, c)
            else:
                @pl.when(jnp.logical_not(same))
                def _():
                    finish(c).start()
    for c in range(chunks):
        sent(1 - PASSES % 2, c)

    @pl.when(jnp.logical_not(same))
    def _():
        pltpu.make_async_copy(out, out, out_recv).wait()
        pltpu.make_async_copy(out, out, out_send).wait()

    pltpu.make_async_copy(others, others, spread_send).wait()


def shards(tile_bounds, tile_anchor, tile_picks, rmo_picks, sensitivity, dip_class, strength, couple):
    tile_count, ray_count, params, tile_z, tile_c = sensitivity.shape
    count = lax.axis_size("cols")
    _, rows_x, rows_y = dip_class.shape
    dma = pltpu.SemaphoreType.DMA
    lines = rows_x * rows_y // 128
    buffer = pltpu.VMEM((2, params, rows_x + 16, rows_y), F32)
    message = pltpu.VMEM((count, params, CAP), F32)
    halo = dma((2, rows_x // CHUNK))
    field = pl.pallas_call(
        step_kernel,
        out_shape=jax.ShapeDtypeStruct((params, rows_x, rows_y), F32),
        in_specs=[SMEM, SMEM, SMEM, SMEM, SMEM, VMEM, VMEM, pl.BlockSpec(memory_space=pl.ANY)],
        out_specs=VMEM,
        scratch_shapes=[
            pltpu.VMEM(sensitivity.shape, sensitivity.dtype),
            pltpu.VMEM((4, 104, 128), F32),
            pltpu.VMEM((384, CAP), F32),
            message,
            message,
            pltpu.VMEM((rows_x, rows_y), jnp.int32),
            pltpu.SMEM((lines + 3,), jnp.int32),
            pltpu.VMEM((4 * count + 4, 8, 128), F32),
            pltpu.VMEM((8 * lines, 128), F32),
            buffer,
            buffer,
            buffer,
            dma,
            dma((3,)),
            dma((3,)),
            dma,
            dma,
            dma,
            dma,
            halo,
            halo,
            halo,
            halo,
            dma,
            dma,
        ],
        compiler_params=pltpu.CompilerParams(collective_id=0, has_side_effects=True),
        name="step",
    )(
        tile_bounds, tile_anchor, tile_picks, strength, couple, rmo_picks, dip_class.reshape(rows_x, rows_y), sensitivity
    )
    return field.reshape(params, 1, rows_x, rows_y)


def solution(mesh):
    return jax.shard_map(
        shards,
        mesh=mesh,
        in_specs=(
            P(),
            P(("cols", "par"), None),
            P(("cols", "par")),
            P(("cols", "par"), None),
            P(("cols", "par"), None, None, None, None),
            P(("cols", "par"), None, None),
            P(),
            P(),
        ),
        out_specs=P(None, ("cols", "par"), None, None),
        check_vma=False,
    )
```

time: 625 us -> 62.2 us (0.10)
  waiting for transfers between devices: 442 us -> 0 us
  local copies, waits for them, and re-layouts: 103 us -> 1.62 us
  Pallas kernels: 0 us -> 59.3 us
  starting transfers between devices: 40.9 us -> 0 us
  between operations: 13.8 us -> 0.01 us
  matrix products: 8.09 us -> 0 us
  loops' own time: 7.5 us -> 0 us
    reduce_scatter x1 -> x0, waiting for transfers between devices: 356 us -> none  [shards(): summed = lax.psum_scatter(moved, 'par', scatter_dimension=2, tiled=True)]
    gather x2 -> x0, local copies, waits for them, and re-layouts: 64.4 us -> none  [shards(): jnp.take(padded_slots, slot_index, axis=2)]
    pallas_call x0 -> x1, Pallas kernels: none -> 59.3 us  [shards(): pl.pallas_call(step_kernel, out_shape=jax.ShapeDtypeStruct((params, rows_...]
    ppermute x12 -> x0, waiting for transfers between devices: 57.6 us -> none  [the longest x6 48.2 us: extended(): lax.ppermute(lax.slice_in_dim(block, block.shape[dim] - width, None, axis...]
    all_to_all x1 -> x0, waiting for transfers between devices: 29 us -> none  [shards(): lax.all_to_all(blocks, 'cols', split_axis=1, concat_axis=4, tiled=True)]
    ppermute x12 -> x0, starting transfers between devices: 28.1 us -> none  [the longest x6 14.3 us: extended(): lax.ppermute(lax.slice_in_dim(block, 0, width, axis=dim), axis, backward)]
    all_to_all x1 -> x0, local copies, waits for them, and re-layouts: 23.2 us -> none  [shards(): lax.all_to_all(blocks, 'cols', split_axis=1, concat_axis=4, tiled=True)]
    all_to_all x1 -> x0, starting transfers between devices: 12.7 us -> none  [shards(): lax.all_to_all(blocks, 'cols', split_axis=1, concat_axis=4, tiled=True)]
  transfers between devices with their start and end apart: 14 -> 0, of which waited for: 14 -> 0; matrix products, arithmetic and copies ran while one was open for 0% -> 0% of each run, Pallas kernels for 0% -> 0%
where the time goes in v2:
time: 62.2 us; the launch traced here: 60.9 us
  Pallas kernels  59.3 us (95%)
  local copies, waits for them, and re-layouts  1.62 us (3%)
    pallas_call x1, Pallas kernels, shards(): pl.pallas_call(step_kernel, out_shape=jax.ShapeDtypeStruct((params, rows_...  59.3 us
    unnamed x1, local copies, waits for them, and re-layouts  1.62 us

profile of v2, /device:TPU:32, one launch (start us, length us, event | category | flops | bytes accessed | tf_op | source)
XLA Modules:
  0.0 60.9 jit_solution(4480516242162009456)
XLA Ops:
  0.0 59.3 %step.1 = f32[3,64,256]{2,1,0:T(8,128)} custom-call(s32[65]{0:T(128)} %bounds.1, s32[2,2]{1,0:T(2,128)} %anchor.1, s32[2]{0:T(128)} %picks.1, f32[3]{0:T(128)} %strength.1, f32[3,3]{1,0:T(4,128)} %couple.1, bf16[2,64]{1,0:T(2,128)(2,1)} %rmo.1, s32[64,256]{1,0:T(8,128)} %bitcast.5, bf16[2,64,3,16,128]{4,3,2,1,0:T(8,128)(2,1)} %sens_in.1), custom_call_target="tpu_custom_call" | custom-call | tf_op jit(solution)/shard_map/step/pallas_call | solution.py:345
  59.3 1.6 %copy.11 = f32[3,1,64,256]{3,2,1,0:T(8,128)} copy(f32[3,1,64,256]{3,2,1,0:T(8,128)} %bitcast.4) | data formatting | bytes 393216

commit v3 on v2

--- a/solution.py
+++ b/solution.py
@@ -38,11 +38,11 @@
 def step_kernel(
     bounds, anchor, picks, strength, couple, rmo, dip_in, sens_in, out,
     sens, tiles, placed, rows, spread, dip, table, rolled, stage, fields, below, above,
-    sens_sem, share_send, share_recv, spread_send, spread_recv, dip_send, dip_recv,
+    ready, sens_sem, share_send, share_recv, spread_send, spread_recv, dip_send, dip_recv,
     sends_up, recvs_up, sends_down, recvs_down, out_send, out_recv,
 ):
     cols, par = lax.axis_index("cols"), lax.axis_index("par")
-    count = spread.shape[0]
+    count = lax.axis_size("cols")
     params, rows_x, rows_y = out.shape
     chunks = rows_x // CHUNK
     layer, layers = layer_of(cols, par), 4 * count
@@ -58,11 +58,12 @@
     load.start()
     barrier = pltpu.get_barrier_semaphore()
 
-    def greet(step, carry):
-        pl.semaphore_signal(barrier, inc=1, **to((cols + step) % count, par))
-        return carry
-
-    lax.fori_loop(1, count, greet, 0)
+    plane, spot = cols // 8, cols % 8
+    planes = count // 8
+    for step in range(1, planes):
+        pl.semaphore_signal(barrier, inc=1, **to(8 * ((plane + step) % planes) + spot, par))
+    for step in range(1, 8):
+        pl.semaphore_signal(barrier, inc=1, **to(8 * plane + (spot + step) % 8, par))
     for step in (1, 2, 3):
         pl.semaphore_signal(barrier, inc=1, **to(cols, (par + step) % 4))
 
@@ -123,7 +124,7 @@
     tiles[0, pl.ds(96, 8), :] = facts
 
     remote_pairs = jnp.where(same, 0, 2)
-    pl.semaphore_wait(barrier, count + 2 + remote_pairs + jnp.where(has_down, 1, 0) + jnp.where(has_up, 1, 0))
+    pl.semaphore_wait(barrier, planes + 9 + remote_pairs + jnp.where(has_down, 1, 0) + jnp.where(has_up, 1, 0))
 
     shares = [
         pltpu.make_async_remote_copy(
@@ -133,6 +134,8 @@
     ]
     for share in (shares[1], shares[2], shares[0]):
         share.start()
+    for step in range(1, planes):
+        pl.semaphore_signal(ready, inc=1, **to(8 * ((plane + step) % planes) + spot, par))
     dip_copy = pltpu.make_async_remote_copy(dip_in, dip, dip_send, dip_recv, **to(holder_cols, holder_par))
 
     @pl.when(other)
@@ -174,15 +177,21 @@
         total += jnp.dot(match, piece, preferred_element_type=F32)
         value = value - piece.astype(F32)
     for c in range(count):
-        rows[c] = total[4 * c : 4 * c + params]
+        for k in range(3):
+            rows[pl.ds(9 * c + 3 * k, 3), :] = total[4 * c : 4 * c + params, 128 * k : 128 * (k + 1)]
+
+    pl.semaphore_wait(ready, planes - 1)
 
     def put(i, carry):
-        peer = (cols + (i + count // 2 - 1) % (count - 1) + 1) % count
-        pltpu.make_async_remote_copy(rows.at[peer], spread.at[cols], spread_send, spread_recv, **to(peer, par)).start()
+        step = (i % planes) * 8 + i // planes
+        peer = (cols + step) % count
+        pltpu.make_async_remote_copy(
+            rows.at[pl.ds(9 * peer, 9)], spread.at[pl.ds(9 * cols, 9)], spread_send, spread_recv, **to(peer, par)
+        ).start()
         return carry
 
-    lax.fori_loop(0, count - 1, put, 0)
-    spread[cols] = rows[cols]
+    lax.fori_loop(1, count, put, 0)
+    spread[pl.ds(9 * cols, 9)] = rows[pl.ds(9 * cols, 9)]
 
     at_y = lax.broadcasted_iota(jnp.int32, (CHUNK, rows_y), 1)
     west_edge, east_edge = at_y == 0, at_y == rows_y - 1
@@ -241,19 +250,17 @@
     def pick(lower, higher, low, mid, high):
         return jnp.where(lower, low, jnp.where(higher, high, mid))
 
-    others = spread.at[pl.ds(0, count - 1)]
+    others = spread.at[pl.ds(0, 9 * (count - 1))]
     pltpu.make_async_copy(others, others, spread_recv).wait()
 
     lane = lax.broadcasted_iota(jnp.int32, (8, 128), 1)
-    blank = jnp.zeros((8 - params, 128), F32)
 
     def turn(c, carry):
         fine = bounds[c] % 128
         before = jnp.zeros((8, 128), F32)
         for k in range(4):
             if k < 3:
-                part = jnp.concatenate([spread[c, :, pl.ds(128 * k, 128)], blank], axis=0)
-                part = pltpu.roll(part, fine, 1)
+                part = pltpu.roll(spread[pl.ds(9 * c + 3 * k, 8), :], fine, 1)
             else:
                 part = jnp.zeros((8, 128), F32)
             rolled[4 * c + k] = jnp.where(lane >= fine, part, before)
@@ -340,7 +347,7 @@
     dma = pltpu.SemaphoreType.DMA
     lines = rows_x * rows_y // 128
     buffer = pltpu.VMEM((2, params, rows_x + 16, rows_y), F32)
-    message = pltpu.VMEM((count, params, CAP), F32)
+    message = pltpu.VMEM((9 * count + 8, 128), F32)
     halo = dma((2, rows_x // CHUNK))
     field = pl.pallas_call(
         step_kernel,
@@ -360,6 +367,7 @@
             buffer,
             buffer,
             buffer,
+            pltpu.SemaphoreType.REGULAR,
             dma,
             dma((3,)),
             dma((3,)),

time: 62.2 us -> 58.5 us (0.941)
  the two profiles are of different devices: /device:TPU:32 before, /device:TPU:34 now
where the time goes in v3:
time: 58.5 us; the launch traced here: 58.3 us
  Pallas kernels  56.7 us (97%)
  local copies, waits for them, and re-layouts  1.62 us (3%)
    pallas_call x1, Pallas kernels, shards(): pl.pallas_call(step_kernel, out_shape=jax.ShapeDtypeStruct((params, rows_...  56.7 us
    unnamed x1, local copies, waits for them, and re-layouts  1.62 us

profile of v3, /device:TPU:34, one launch (start us, length us, event | category | flops | bytes accessed | tf_op | source)
XLA Modules:
  0.0 58.3 jit_solution(5307374229858243887)
XLA Ops:
  0.0 56.7 %step.1 = f32[3,64,256]{2,1,0:T(8,128)} custom-call(s32[65]{0:T(128)} %bounds.1, s32[2,2]{1,0:T(2,128)} %anchor.1, s32[2]{0:T(128)} %picks.1, f32[3]{0:T(128)} %strength.1, f32[3,3]{1,0:T(4,128)} %couple.1, bf16[2,64]{1,0:T(2,128)(2,1)} %rmo.1, s32[64,256]{1,0:T(8,128)} %bitcast.5, bf16[2,64,3,16,128]{4,3,2,1,0:T(8,128)(2,1)} %sens_in.1), custom_call_target="tpu_custom_call" | custom-call | tf_op jit(solution)/shard_map/step/pallas_call | solution.py:352
  56.7 1.6 %copy.11 = f32[3,1,64,256]{3,2,1,0:T(8,128)} copy(f32[3,1,64,256]{3,2,1,0:T(8,128)} %bitcast.4) | data formatting | bytes 393216

commit v4 on v3

--- a/solution.py
+++ b/solution.py
@@ -14,21 +14,20 @@
 
 
 def layer_of(cols, par):
-    plane, y_lo, x = cols // 8, (cols // 4) % 2, cols % 4
-    y_hi, core = par // 2, par % 2
-    place = 4 * (2 * y_hi + y_lo) + x + y_lo * (3 - 2 * x)
-    place = place + (plane % 2) * (15 - 2 * place)
-    return 32 * plane + 2 * place + core
+    plane, x = cols // 8, cols % 4
+    y, core = 2 * (par // 2) + (cols // 4) % 2, par % 2
+    middle, turn = ((y + 1) // 2) % 2, (y + 1) % 2
+    place = 2 * x + (turn + x) % 2
+    half = (middle + (place + 1) // 8) % 2
+    return 32 * plane + 2 * (8 * half + place) + core
 
 
 def holder_of(layer):
-    plane, rest = layer // 32, layer % 32
-    place, core = rest // 2, rest % 2
-    place = place + (plane % 2) * (15 - 2 * place)
-    y, x = place // 4, place % 4
-    y_lo = y % 2
-    x = x + y_lo * (3 - 2 * x)
-    return 8 * plane + 4 * y_lo + x, 2 * (y // 2) + core
+    plane, core = layer // 32, layer % 2
+    half, place = (layer // 16) % 2, (layer // 2) % 8
+    middle, turn = (half + (place + 1) // 8) % 2, ((place + 1) // 2) % 2
+    y = (1 - middle) * 3 * (1 - turn) + middle * (1 + turn)
+    return 8 * plane + 4 * (y % 2) + place // 2, 2 * (y // 2) + core
 
 
 def to(cols, par):
@@ -138,14 +137,6 @@
         pl.semaphore_signal(ready, inc=1, **to(8 * ((plane + step) % planes) + spot, par))
     dip_copy = pltpu.make_async_remote_copy(dip_in, dip, dip_send, dip_recv, **to(holder_cols, holder_par))
 
-    @pl.when(other)
-    def _():
-        dip_copy.start()
-
-    @pl.when(same)
-    def _():
-        dip[...] = dip_in[...]
-
     place = lax.broadcasted_iota(jnp.int32, (4 * count, 384), 0)
     item = lax.broadcasted_iota(jnp.int32, (4 * count, 384), 1)
     wanted = jnp.where(place % 4 == (item // 16) % 3, layer_of(place // 4, par) - item % 16, -1).astype(F32)
@@ -191,6 +182,15 @@
         return carry
 
     lax.fori_loop(1, count, put, 0)
+
+    @pl.when(other)
+    def _():
+        dip_copy.start()
+
+    @pl.when(same)
+    def _():
+        dip[...] = dip_in[...]
+
     spread[pl.ds(9 * cols, 9)] = rows[pl.ds(9 * cols, 9)]
 
     at_y = lax.broadcasted_iota(jnp.int32, (CHUNK, rows_y), 1)

time: 58.5 us -> 57.8 us (0.988)
  the two profiles are of different devices: /device:TPU:34 before, /device:TPU:32 now
where the time goes in v4:
time: 57.8 us; the launch traced here: 57.7 us
  Pallas kernels  56.1 us (97%)
  local copies, waits for them, and re-layouts  1.62 us (3%)
    pallas_call x1, Pallas kernels, shards(): pl.pallas_call(step_kernel, out_shape=jax.ShapeDtypeStruct((params, rows_...  56.1 us
    unnamed x1, local copies, waits for them, and re-layouts  1.62 us

profile of v4, /device:TPU:32, one launch (start us, length us, event | category | flops | bytes accessed | tf_op | source)
XLA Modules:
  0.0 57.7 jit_solution(17560803840209189604)
XLA Ops:
  0.0 56.1 %step.1 = f32[3,64,256]{2,1,0:T(8,128)} custom-call(s32[65]{0:T(128)} %bounds.1, s32[2,2]{1,0:T(2,128)} %anchor.1, s32[2]{0:T(128)} %picks.1, f32[3]{0:T(128)} %strength.1, f32[3,3]{1,0:T(4,128)} %couple.1, bf16[2,64]{1,0:T(2,128)(2,1)} %rmo.1, s32[64,256]{1,0:T(8,128)} %bitcast.5, bf16[2,64,3,16,128]{4,3,2,1,0:T(8,128)(2,1)} %sens_in.1), custom_call_target="tpu_custom_call" | custom-call | tf_op jit(solution)/shard_map/step/pallas_call | solution.py:352
  56.1 1.6 %copy.11 = f32[3,1,64,256]{3,2,1,0:T(8,128)} copy(f32[3,1,64,256]{3,2,1,0:T(8,128)} %bitcast.4) | data formatting | bytes 393216

commit v5 on v4

--- a/solution.py
+++ b/solution.py
@@ -351,7 +351,7 @@
     halo = dma((2, rows_x // CHUNK))
     field = pl.pallas_call(
         step_kernel,
-        out_shape=jax.ShapeDtypeStruct((params, rows_x, rows_y), F32),
+        out_shape=pltpu.VMEM((params, rows_x, rows_y), F32),
         in_specs=[SMEM, SMEM, SMEM, SMEM, SMEM, VMEM, VMEM, pl.BlockSpec(memory_space=pl.ANY)],
         out_specs=VMEM,
         scratch_shapes=[

time: 57.8 us -> 56.2 us (0.972)
  local copies, waits for them, and re-layouts: 1.62 us -> 0.68 us
  Pallas kernels: 56.1 us -> 55.4 us
    unnamed x1, local copies, waits for them, and re-layouts: 1.62 us -> 0.68 us
    pallas_call x1, Pallas kernels: 56.1 us -> 55.4 us  [shards(): pl.pallas_call(step_kernel, out_shape=pltpu.VMEM((params, rows_x, rows_y)...]
where the time goes in v5:
time: 56.2 us; the launch traced here: 56.1 us
  Pallas kernels  55.4 us (99%)
  local copies, waits for them, and re-layouts  0.68 us (1%)
    pallas_call x1, Pallas kernels, shards(): pl.pallas_call(step_kernel, out_shape=pltpu.VMEM((params, rows_x, rows_y)...  55.4 us

profile of v5, /device:TPU:32, one launch (start us, length us, event | category | flops | bytes accessed | tf_op | source)
XLA Modules:
  0.0 56.1 jit_solution(10714396294237135629)
XLA Ops:
  0.0 55.4 %step.1 = f32[3,64,256]{2,1,0:T(8,128)S(1)} custom-call(s32[65]{0:T(128)} %bounds.1, s32[2,2]{1,0:T(2,128)} %anchor.1, s32[2]{0:T(128)} %picks.1, f32[3]{0:T(128)} %strength.1, f32[3,3]{1,0:T(4,128)} %couple.1, bf16[2,64]{1,0:T(2,128)(2,1)} %rmo.1, s32[64,256]{1,0:T(8,128)} %bitcast.5, bf16[2,64,3,16,128]{4,3,2,1,0:T(8,128)(2,1)} %sens_in.1), custom_call_target="tpu_custom_call" | custom-call | tf_op jit(solution)/shard_map/step/pallas_call | solution.py:352
  55.4 0.7 %copy.11 = f32[3,1,64,256]{3,2,1,0:T(8,128)} copy(f32[3,1,64,256]{3,2,1,0:T(8,128)S(1)} %bitcast.4) | data formatting | bytes 393216
